TPU v7x, 32 devices: a whole 2x2x4 slice. The times are simulated.
32 devices in a mesh: row: 4 (over x, core), col: 8 (over z, y).
Axes of the slice: x: 2, y: 2, z: 4, core: 2. Of those that a mesh axis runs over, the one named last changes fastest.
Arguments:
- optical_field: float32 [2, 512, 4096], P(None, 'row', 'col'), may hold values from -6 to 6
- index_panels: bfloat16 [5, 512, 4096], P(None, ('row', 'col')), may hold values from -4 to 4
Outputs:
- propagated: float32 [2, 512, 4096], P(None, 'row', 'col')
All inputs are finite; a program needn't handle non-finite values.
Results may differ from a plain program's by a relative error of at most 0.0003.
Values may be sent and summed in bfloat16 or wider, within the bound.
A program may use at most 64 MiB of HBM per device.

v0:
```python
import jax
import jax.numpy as jnp
from jax import lax
from jax.sharding import PartitionSpec as P

STEPS = 2
diffraction = 0.15
phase_gain = 0.25


def with_halo(cells, sides, width):
    for axis, dim in sides:
        count = lax.axis_size(axis)
        head = lax.slice_in_dim(cells, 0, width, axis=dim)
        tail = lax.slice_in_dim(cells, cells.shape[dim] - width, cells.shape[dim], axis=dim)
        cells = jnp.concatenate(
            [
                lax.ppermute(tail, axis, [(i, (i + 1) % count) for i in range(count)]),
                cells,
                lax.ppermute(head, axis, [((i + 1) % count, i) for i in range(count)]),
            ],
            axis=dim,
        )
    return cells


def laplace(padded):
    centre = padded[:, 2:-2, 2:-2]
    along_y = 16.0 * (padded[:, 1:-3, 2:-2] + padded[:, 3:-1, 2:-2]) - (
        padded[:, :-4, 2:-2] + padded[:, 4:, 2:-2]
    )
    along_x = 16.0 * (padded[:, 2:-2, 1:-3] + padded[:, 2:-2, 3:-1]) - (
        padded[:, 2:-2, :-4] + padded[:, 2:-2, 4:]
    )
    return (along_y + along_x - 60.0 * centre) / 12.0


def slope(padded, plane):
    centre = padded[:, 2:-2, 2:-2]
    total = diffraction * laplace(padded) + phase_gain * plane.astype(jnp.float32) * centre
    return jnp.stack([-total[1], total[0]])


def section_slope(state, plane):
    padded = with_halo(state, (("row", 1), ("col", 2)), 2)
    return slope(padded, plane)


def local(optical_field, index_panels):
    planes_all = lax.all_to_all(index_panels, "col", split_axis=2, concat_axis=1, tiled=True)
    field = optical_field
    planes = None
    for step_index in range(STEPS):
        first = 2 * step_index
        planes = planes_all[first : first + 3]
        first_slope = section_slope(field, planes[0])
        second_slope = section_slope(field + 0.5 * first_slope, planes[1])
        third_slope = section_slope(field + 0.5 * second_slope, planes[1])
        fourth_slope = section_slope(field + third_slope, planes[2])
        field = field + (first_slope + 2.0 * second_slope + 2.0 * third_slope + fourth_slope) / 6.0
    return field


def solution(mesh):
    in_specs = (P(None, "row", "col"), P(None, ("row", "col"), None))
    out_specs = P(None, "row", "col")
    return jax.shard_map(local, mesh=mesh, in_specs=in_specs, out_specs=out_specs, check_vma=False)
```

profile of v0, /device:TPU:0, one launch (start us, length us, event | category | flops | bytes accessed | tf_op | source)
XLA Modules:
  0.0 162.4 jit_solution(11394870547222477419)
XLA Ops:
  0.0 8.1 %copy.10 = bf16[5,16,4096]{1,0,2:T(8,128)(2,1)} copy(bf16[5,16,4096]{2,1,0:T(8,128)(2,1)} %param.3) | data formatting | bytes 1310720 | tf_op args[1]
  8.1 9.1 %reshape.60 = bf16[8,2,20480]{2,1,0:T(2,128)(2,1)} reshape(bf16[4096,5,16]{2,1,0:T(8,128)(2,1)} %bitcast.10) | data formatting | bytes 1310720
  17.2 7.3 %all-to-all-start = ((bf16[8,2,20480]{2,1,0:T(2,128)(2,1)}), bf16[8,2,20480]{2,1,0:T(2,128)(2,1)S(1)}, u32[]{:S(2)}, u32[]{:S(2)}) async-start(bf16[8,2,20480]{2,1,0:T(2,128)(2,1)} %reshape.60), calls=%async_computation | async-start | bytes 1310720 | tf_op jit(solution)/shard_map/all_to_all | solution.py:50
  24.5 1.7 %collective-permute-start.1 = (f32[2,2,512]{2,1,0:T(2,128)S(1)}, f32[2,2,512]{2,1,0:T(2,128)S(1)}, u32[]{:S(2)}, u32[]{:S(2)}) collective-permute-start(f32[2,2,512]{2,1,0:T(2,128)S(1)} %get-tuple-element.72), channel_id=1, source_target_pairs={{8,0},{16,8},{24,16},{0,24},{9,1},{17,9},{25,17},{1,25},{10,2},{18... | collective-permute-start | bytes 24584 | tf_op jit(solution)/shard_map/ppermute | solution.py:20
  26.3 1.3 collective-permute-done
  27.8 2.1 %collective-permute-start.2 = (f32[2,132,2]{2,1,0:T(8,128)S(1)}, f32[2,132,2]{2,1,0:T(8,128)S(1)}, u32[]{:S(2)}, u32[]{:S(2)}) collective-permute-start(f32[2,132,2]{2,1,0:T(8,128)S(1)} %get-tuple-element.40), channel_id=1, source_target_pairs={{0,1},{1,2},{2,3},{3,4},{4,5},{5,6},{6,7},{7,0},{8,9},{9,10},{10,1... | collective-permute-start | bytes 6344 | tf_op jit(solution)/shard_map/ppermute | solution.py:18
  29.8 2.8 %collective-permute-start.3 = (f32[2,132,2]{2,1,0:T(8,128)S(1)}, f32[2,132,2]{2,1,0:T(8,128)S(1)}, u32[]{:S(2)}, u32[]{:S(2)}) collective-permute-start(f32[2,132,2]{2,1,0:T(8,128)S(1)} %get-tuple-element.41), channel_id=1, source_target_pairs={{1,0},{2,1},{3,2},{4,3},{5,4},{6,5},{7,6},{0,7},{9,8},{10,9},{11,1... | collective-permute-start | bytes 6344 | tf_op jit(solution)/shard_map/ppermute | solution.py:20
  32.6 10.5 %collective-permute-done.2 = f32[2,132,2]{2,1,0:T(8,128)S(1)} collective-permute-done((f32[2,132,2]{2,1,0:T(8,128)S(1)}, f32[2,132,2]{2,1,0:T(8,128)S(1)}, u32[]{:S(2)}, u32[]{:S(2)}) %collective-permute-start.2) | collective-permute-done | bytes 2144 | tf_op jit(solution)/shard_map/ppermute | solution.py:18
  43.4 7.3 %reshape.61 = bf16[4096,5,16]{2,1,0:T(8,128)(2,1)} reshape(bf16[8,2,20480]{2,1,0:T(2,128)(2,1)S(1)} %all-to-all-done) | data formatting | bytes 1310720
  50.7 6.4 %copy.17 = bf16[5,16,8,512]{3,2,1,0:T(8,128)(2,1)S(1)} copy(bf16[5,16,8,512]{1,0,3,2:T(8,128)(2,1)} %bitcast.9) | data formatting | bytes 1310720 | tf_op jit(solution)/shard_map/all_to_all | solution.py:50
  58.3 1.7 %collective-permute-start.5 = (f32[2,2,512]{2,1,0:T(2,128)S(1)}, f32[2,2,512]{2,1,0:T(2,128)S(1)}, u32[]{:S(2)}, u32[]{:S(2)}) collective-permute-start(f32[2,2,512]{2,1,0:T(2,128)S(1)} %get-tuple-element.69), channel_id=1, source_target_pairs={{8,0},{16,8},{24,16},{0,24},{9,1},{17,9},{25,17},{1,25},{10,2},{18... | collective-permute-start | bytes 24584 | tf_op jit(solution)/shard_map/ppermute | solution.py:20
  60.0 1.3 collective-permute-done.4
  61.5 2.8 %collective-permute-start.6 = (f32[2,132,2]{2,1,0:T(8,128)S(1)}, f32[2,132,2]{2,1,0:T(8,128)S(1)}, u32[]{:S(2)}, u32[]{:S(2)}) collective-permute-start(f32[2,132,2]{2,1,0:T(8,128)S(1)} %get-tuple-element.36), channel_id=1, source_target_pairs={{0,1},{1,2},{2,3},{3,4},{4,5},{5,6},{6,7},{7,0},{8,9},{9,10},{10,1... | collective-permute-start | bytes 6344 | tf_op jit(solution)/shard_map/ppermute | solution.py:18
  64.3 2.0 %collective-permute-start.7 = (f32[2,132,2]{2,1,0:T(8,128)S(1)}, f32[2,132,2]{2,1,0:T(8,128)S(1)}, u32[]{:S(2)}, u32[]{:S(2)}) collective-permute-start(f32[2,132,2]{2,1,0:T(8,128)S(1)} %get-tuple-element.37), channel_id=1, source_target_pairs={{1,0},{2,1},{3,2},{4,3},{5,4},{6,5},{7,6},{0,7},{9,8},{10,9},{11,1... | collective-permute-start | bytes 6344 | tf_op jit(solution)/shard_map/ppermute | solution.py:20
  66.5 4.4 %collective-permute-done.6 = f32[2,132,2]{2,1,0:T(8,128)S(1)} collective-permute-done((f32[2,132,2]{2,1,0:T(8,128)S(1)}, f32[2,132,2]{2,1,0:T(8,128)S(1)}, u32[]{:S(2)}, u32[]{:S(2)}) %collective-permute-start.6) | collective-permute-done | bytes 2144 | tf_op jit(solution)/shard_map/ppermute | solution.py:18
  70.8 2.9 %collective-permute-done.7 = f32[2,132,2]{2,1,0:T(8,128)S(1)} collective-permute-done((f32[2,132,2]{2,1,0:T(8,128)S(1)}, f32[2,132,2]{2,1,0:T(8,128)S(1)}, u32[]{:S(2)}, u32[]{:S(2)}) %collective-permute-start.7) | collective-permute-done | bytes 2144 | tf_op jit(solution)/shard_map/ppermute | solution.py:20
  74.1 0.6 fusion.61
  75.0 1.6 %collective-permute-start.9 = (f32[2,2,512]{2,1,0:T(2,128)S(1)}, f32[2,2,512]{2,1,0:T(2,128)S(1)}, u32[]{:S(2)}, u32[]{:S(2)}) collective-permute-start(f32[2,2,512]{2,1,0:T(2,128)S(1)} %get-tuple-element.65), channel_id=1, source_target_pairs={{8,0},{16,8},{24,16},{0,24},{9,1},{17,9},{25,17},{1,25},{10,2},{18... | collective-permute-start | bytes 24584 | tf_op jit(solution)/shard_map/ppermute | solution.py:20
  76.7 1.3 collective-permute-done.8
  78.2 4.7 %collective-permute-start.11 = (f32[2,132,2]{2,1,0:T(8,128)S(1)}, f32[2,132,2]{2,1,0:T(8,128)S(1)}, u32[]{:S(2)}, u32[]{:S(2)}) collective-permute-start(f32[2,132,2]{2,1,0:T(8,128)S(1)} %get-tuple-element.33), channel_id=1, source_target_pairs={{1,0},{2,1},{3,2},{4,3},{5,4},{6,5},{7,6},{0,7},{9,8},{10,9},{11,1... | collective-permute-start | bytes 6344 | tf_op jit(solution)/shard_map/ppermute | solution.py:20
  82.9 4.6 %collective-permute-done.10 = f32[2,132,2]{2,1,0:T(8,128)S(1)} collective-permute-done((f32[2,132,2]{2,1,0:T(8,128)S(1)}, f32[2,132,2]{2,1,0:T(8,128)S(1)}, u32[]{:S(2)}, u32[]{:S(2)}) %collective-permute-start.10) | collective-permute-done | bytes 2144 | tf_op jit(solution)/shard_map/ppermute | solution.py:18
  88.1 0.6 fusion.52
  89.0 1.6 %collective-permute-start.13 = (f32[2,2,512]{2,1,0:T(2,128)S(1)}, f32[2,2,512]{2,1,0:T(2,128)S(1)}, u32[]{:S(2)}, u32[]{:S(2)}) collective-permute-start(f32[2,2,512]{2,1,0:T(2,128)S(1)} %get-tuple-element.61), channel_id=1, source_target_pairs={{8,0},{16,8},{24,16},{0,24},{9,1},{17,9},{25,17},{1,25},{10,2},{18... | collective-permute-start | bytes 24584 | tf_op jit(solution)/shard_map/ppermute | solution.py:20
  90.6 1.3 collective-permute-done.12
  92.2 4.7 %collective-permute-start.15 = (f32[2,132,2]{2,1,0:T(8,128)S(1)}, f32[2,132,2]{2,1,0:T(8,128)S(1)}, u32[]{:S(2)}, u32[]{:S(2)}) collective-permute-start(f32[2,132,2]{2,1,0:T(8,128)S(1)} %get-tuple-element.29), channel_id=1, source_target_pairs={{1,0},{2,1},{3,2},{4,3},{5,4},{6,5},{7,6},{0,7},{9,8},{10,9},{11,1... | collective-permute-start | bytes 6344 | tf_op jit(solution)/shard_map/ppermute | solution.py:20
  97.1 4.2 %collective-permute-done.14 = f32[2,132,2]{2,1,0:T(8,128)S(1)} collective-permute-done((f32[2,132,2]{2,1,0:T(8,128)S(1)}, f32[2,132,2]{2,1,0:T(8,128)S(1)}, u32[]{:S(2)}, u32[]{:S(2)}) %collective-permute-start.14) | collective-permute-done | bytes 2144 | tf_op jit(solution)/shard_map/ppermute | solution.py:18
  101.5 0.6 fusion.43
  102.9 1.4 collective-permute-start.17
  104.3 1.3 collective-permute-done.16
  105.9 5.1 %collective-permute-start.19 = (f32[2,132,2]{2,1,0:T(8,128)S(1)}, f32[2,132,2]{2,1,0:T(8,128)S(1)}, u32[]{:S(2)}, u32[]{:S(2)}) collective-permute-start(f32[2,132,2]{2,1,0:T(8,128)S(1)} %get-tuple-element.25), channel_id=1, source_target_pairs={{1,0},{2,1},{3,2},{4,3},{5,4},{6,5},{7,6},{0,7},{9,8},{10,9},{11,1... | collective-permute-start | bytes 6344 | tf_op jit(solution)/shard_map/ppermute | solution.py:20
  111.0 3.8 %collective-permute-done.18 = f32[2,132,2]{2,1,0:T(8,128)S(1)} collective-permute-done((f32[2,132,2]{2,1,0:T(8,128)S(1)}, f32[2,132,2]{2,1,0:T(8,128)S(1)}, u32[]{:S(2)}, u32[]{:S(2)}) %collective-permute-start.18) | collective-permute-done | bytes 2144 | tf_op jit(solution)/shard_map/ppermute | solution.py:18
  116.9 1.3 collective-permute-start.21
  118.1 1.3 collective-permute-done.20
  119.7 5.3 %collective-permute-start.23 = (f32[2,132,2]{2,1,0:T(8,128)S(1)}, f32[2,132,2]{2,1,0:T(8,128)S(1)}, u32[]{:S(2)}, u32[]{:S(2)}) collective-permute-start(f32[2,132,2]{2,1,0:T(8,128)S(1)} %get-tuple-element.21), channel_id=1, source_target_pairs={{1,0},{2,1},{3,2},{4,3},{5,4},{6,5},{7,6},{0,7},{9,8},{10,9},{11,1... | collective-permute-start | bytes 6344 | tf_op jit(solution)/shard_map/ppermute | solution.py:20
  125.1 3.9 %collective-permute-done.22 = f32[2,132,2]{2,1,0:T(8,128)S(1)} collective-permute-done((f32[2,132,2]{2,1,0:T(8,128)S(1)}, f32[2,132,2]{2,1,0:T(8,128)S(1)}, u32[]{:S(2)}, u32[]{:S(2)}) %collective-permute-start.22) | collective-permute-done | bytes 2144 | tf_op jit(solution)/shard_map/ppermute | solution.py:18
  129.0 0.9 collective-permute-done.23
  130.2 0.6 fusion.25
  131.4 1.6 %collective-permute-start.25 = (f32[2,2,512]{2,1,0:T(2,128)S(1)}, f32[2,2,512]{2,1,0:T(2,128)S(1)}, u32[]{:S(2)}, u32[]{:S(2)}) collective-permute-start(f32[2,2,512]{2,1,0:T(2,128)S(1)} %get-tuple-element.49), channel_id=1, source_target_pairs={{8,0},{16,8},{24,16},{0,24},{9,1},{17,9},{25,17},{1,25},{10,2},{18... | collective-permute-start | bytes 24584 | tf_op jit(solution)/shard_map/ppermute | solution.py:20
  133.0 1.3 collective-permute-done.24
  134.7 4.5 %collective-permute-start.27 = (f32[2,132,2]{2,1,0:T(8,128)S(1)}, f32[2,132,2]{2,1,0:T(8,128)S(1)}, u32[]{:S(2)}, u32[]{:S(2)}) collective-permute-start(f32[2,132,2]{2,1,0:T(8,128)S(1)} %get-tuple-element.17), channel_id=1, source_target_pairs={{1,0},{2,1},{3,2},{4,3},{5,4},{6,5},{7,6},{0,7},{9,8},{10,9},{11,1... | collective-permute-start | bytes 6344 | tf_op jit(solution)/shard_map/ppermute | solution.py:20
  139.3 4.2 %collective-permute-done.26 = f32[2,132,2]{2,1,0:T(8,128)S(1)} collective-permute-done((f32[2,132,2]{2,1,0:T(8,128)S(1)}, f32[2,132,2]{2,1,0:T(8,128)S(1)}, u32[]{:S(2)}, u32[]{:S(2)}) %collective-permute-start.26) | collective-permute-done | bytes 2144 | tf_op jit(solution)/shard_map/ppermute | solution.py:18
  143.5 1.5 collective-permute-done.27
  146.5 1.6 %collective-permute-start.29 = (f32[2,2,512]{2,1,0:T(2,128)S(1)}, f32[2,2,512]{2,1,0:T(2,128)S(1)}, u32[]{:S(2)}, u32[]{:S(2)}) collective-permute-start(f32[2,2,512]{2,1,0:T(2,128)S(1)} %get-tuple-element.45), channel_id=1, source_target_pairs={{8,0},{16,8},{24,16},{0,24},{9,1},{17,9},{25,17},{1,25},{10,2},{18... | collective-permute-start | bytes 24584 | tf_op jit(solution)/shard_map/ppermute | solution.py:20
  148.1 1.3 collective-permute-done.28
  149.8 4.5 %collective-permute-start.31 = (f32[2,132,2]{2,1,0:T(8,128)S(1)}, f32[2,132,2]{2,1,0:T(8,128)S(1)}, u32[]{:S(2)}, u32[]{:S(2)}) collective-permute-start(f32[2,132,2]{2,1,0:T(8,128)S(1)} %get-tuple-element.13), channel_id=1, source_target_pairs={{1,0},{2,1},{3,2},{4,3},{5,4},{6,5},{7,6},{0,7},{9,8},{10,9},{11,1... | collective-permute-start | bytes 6344 | tf_op jit(solution)/shard_map/ppermute | solution.py:20
  154.5 4.0 %collective-permute-done.30 = f32[2,132,2]{2,1,0:T(8,128)S(1)} collective-permute-done((f32[2,132,2]{2,1,0:T(8,128)S(1)}, f32[2,132,2]{2,1,0:T(8,128)S(1)}, u32[]{:S(2)}, u32[]{:S(2)}) %collective-permute-start.30) | collective-permute-done | bytes 2144 | tf_op jit(solution)/shard_map/ppermute | solution.py:18
  158.6 1.5 collective-permute-done.31
  161.0 1.4 fusion.97
  (80 shorter events, 11.9 us)
Async XLA Ops:
  0.0 24.5 %copy-start = (f32[2,128,512]{2,1,0:T(8,128)S(1)}, f32[2,128,512]{2,1,0:T(8,128)}, u32[]{:S(2)}) copy-start(f32[2,128,512]{2,1,0:T(8,128)} %param.2) | copy-start | bytes 1572868
  17.2 26.2 %all-to-all-start = ((bf16[8,2,20480]{2,1,0:T(2,128)(2,1)}), bf16[8,2,20480]{2,1,0:T(2,128)(2,1)S(1)}, u32[]{:S(2)}, u32[]{:S(2)}) async-start(bf16[8,2,20480]{2,1,0:T(2,128)(2,1)} %reshape.60), calls=%async_computation | async-start | bytes 1310720 | tf_op jit(solution)/shard_map/all_to_all | solution.py:50
  24.5 3.1 %collective-permute-start = (f32[2,2,512]{2,1,0:T(2,128)S(1)}, f32[2,2,512]{2,1,0:T(2,128)S(1)}, u32[]{:S(2)}, u32[]{:S(2)}) collective-permute-start(f32[2,2,512]{2,1,0:T(2,128)S(1)} %get-tuple-element.73), channel_id=1, source_target_pairs={{0,8},{8,16},{16,24},{24,0},{1,9},{9,17},{17,25},{25,1},{2,10},{10... | collective-permute-start | bytes 24584 | tf_op jit(solution)/shard_map/ppermute | solution.py:18
  24.5 3.1 %collective-permute-start.1 = (f32[2,2,512]{2,1,0:T(2,128)S(1)}, f32[2,2,512]{2,1,0:T(2,128)S(1)}, u32[]{:S(2)}, u32[]{:S(2)}) collective-permute-start(f32[2,2,512]{2,1,0:T(2,128)S(1)} %get-tuple-element.72), channel_id=1, source_target_pairs={{8,0},{16,8},{24,16},{0,24},{9,1},{17,9},{25,17},{1,25},{10,2},{18... | collective-permute-start | bytes 24584 | tf_op jit(solution)/shard_map/ppermute | solution.py:20
  27.8 15.4 %collective-permute-start.2 = (f32[2,132,2]{2,1,0:T(8,128)S(1)}, f32[2,132,2]{2,1,0:T(8,128)S(1)}, u32[]{:S(2)}, u32[]{:S(2)}) collective-permute-start(f32[2,132,2]{2,1,0:T(8,128)S(1)} %get-tuple-element.40), channel_id=1, source_target_pairs={{0,1},{1,2},{2,3},{3,4},{4,5},{5,6},{6,7},{7,0},{8,9},{9,10},{10,1... | collective-permute-start | bytes 6344 | tf_op jit(solution)/shard_map/ppermute | solution.py:18
  29.8 13.3 %collective-permute-start.3 = (f32[2,132,2]{2,1,0:T(8,128)S(1)}, f32[2,132,2]{2,1,0:T(8,128)S(1)}, u32[]{:S(2)}, u32[]{:S(2)}) collective-permute-start(f32[2,132,2]{2,1,0:T(8,128)S(1)} %get-tuple-element.41), channel_id=1, source_target_pairs={{1,0},{2,1},{3,2},{4,3},{5,4},{6,5},{7,6},{0,7},{9,8},{10,9},{11,1... | collective-permute-start | bytes 6344 | tf_op jit(solution)/shard_map/ppermute | solution.py:20
  58.2 3.1 %collective-permute-start.4 = (f32[2,2,512]{2,1,0:T(2,128)S(1)}, f32[2,2,512]{2,1,0:T(2,128)S(1)}, u32[]{:S(2)}, u32[]{:S(2)}) collective-permute-start(f32[2,2,512]{2,1,0:T(2,128)S(1)} %get-tuple-element.68), channel_id=1, source_target_pairs={{0,8},{8,16},{16,24},{24,0},{1,9},{9,17},{17,25},{25,1},{2,10},{10... | collective-permute-start | bytes 24584 | tf_op jit(solution)/shard_map/ppermute | solution.py:18
  58.3 3.1 %collective-permute-start.5 = (f32[2,2,512]{2,1,0:T(2,128)S(1)}, f32[2,2,512]{2,1,0:T(2,128)S(1)}, u32[]{:S(2)}, u32[]{:S(2)}) collective-permute-start(f32[2,2,512]{2,1,0:T(2,128)S(1)} %get-tuple-element.69), channel_id=1, source_target_pairs={{8,0},{16,8},{24,16},{0,24},{9,1},{17,9},{25,17},{1,25},{10,2},{18... | collective-permute-start | bytes 24584 | tf_op jit(solution)/shard_map/ppermute | solution.py:20
  61.5 9.3 %collective-permute-start.6 = (f32[2,132,2]{2,1,0:T(8,128)S(1)}, f32[2,132,2]{2,1,0:T(8,128)S(1)}, u32[]{:S(2)}, u32[]{:S(2)}) collective-permute-start(f32[2,132,2]{2,1,0:T(8,128)S(1)} %get-tuple-element.36), channel_id=1, source_target_pairs={{0,1},{1,2},{2,3},{3,4},{4,5},{5,6},{6,7},{7,0},{8,9},{9,10},{10,1... | collective-permute-start | bytes 6344 | tf_op jit(solution)/shard_map/ppermute | solution.py:18
  64.3 9.4 %collective-permute-start.7 = (f32[2,132,2]{2,1,0:T(8,128)S(1)}, f32[2,132,2]{2,1,0:T(8,128)S(1)}, u32[]{:S(2)}, u32[]{:S(2)}) collective-permute-start(f32[2,132,2]{2,1,0:T(8,128)S(1)} %get-tuple-element.37), channel_id=1, source_target_pairs={{1,0},{2,1},{3,2},{4,3},{5,4},{6,5},{7,6},{0,7},{9,8},{10,9},{11,1... | collective-permute-start | bytes 6344 | tf_op jit(solution)/shard_map/ppermute | solution.py:20
  74.9 3.1 %collective-permute-start.8 = (f32[2,2,512]{2,1,0:T(2,128)S(1)}, f32[2,2,512]{2,1,0:T(2,128)S(1)}, u32[]{:S(2)}, u32[]{:S(2)}) collective-permute-start(f32[2,2,512]{2,1,0:T(2,128)S(1)} %get-tuple-element.64), channel_id=1, source_target_pairs={{0,8},{8,16},{16,24},{24,0},{1,9},{9,17},{17,25},{25,1},{2,10},{10... | collective-permute-start | bytes 24584 | tf_op jit(solution)/shard_map/ppermute | solution.py:18
  75.0 3.0 %collective-permute-start.9 = (f32[2,2,512]{2,1,0:T(2,128)S(1)}, f32[2,2,512]{2,1,0:T(2,128)S(1)}, u32[]{:S(2)}, u32[]{:S(2)}) collective-permute-start(f32[2,2,512]{2,1,0:T(2,128)S(1)} %get-tuple-element.65), channel_id=1, source_target_pairs={{8,0},{16,8},{24,16},{0,24},{9,1},{17,9},{25,17},{1,25},{10,2},{18... | collective-permute-start | bytes 24584 | tf_op jit(solution)/shard_map/ppermute | solution.py:20
  78.2 9.3 %collective-permute-start.10 = (f32[2,132,2]{2,1,0:T(8,128)S(1)}, f32[2,132,2]{2,1,0:T(8,128)S(1)}, u32[]{:S(2)}, u32[]{:S(2)}) collective-permute-start(f32[2,132,2]{2,1,0:T(8,128)S(1)} %get-tuple-element.32), channel_id=1, source_target_pairs={{0,1},{1,2},{2,3},{3,4},{4,5},{5,6},{6,7},{7,0},{8,9},{9,10},{10,1... | collective-permute-start | bytes 6344 | tf_op jit(solution)/shard_map/ppermute | solution.py:18
  78.2 9.5 %collective-permute-start.11 = (f32[2,132,2]{2,1,0:T(8,128)S(1)}, f32[2,132,2]{2,1,0:T(8,128)S(1)}, u32[]{:S(2)}, u32[]{:S(2)}) collective-permute-start(f32[2,132,2]{2,1,0:T(8,128)S(1)} %get-tuple-element.33), channel_id=1, source_target_pairs={{1,0},{2,1},{3,2},{4,3},{5,4},{6,5},{7,6},{0,7},{9,8},{10,9},{11,1... | collective-permute-start | bytes 6344 | tf_op jit(solution)/shard_map/ppermute | solution.py:20
  88.8 3.1 %collective-permute-start.12 = (f32[2,2,512]{2,1,0:T(2,128)S(1)}, f32[2,2,512]{2,1,0:T(2,128)S(1)}, u32[]{:S(2)}, u32[]{:S(2)}) collective-permute-start(f32[2,2,512]{2,1,0:T(2,128)S(1)} %get-tuple-element.60), channel_id=1, source_target_pairs={{0,8},{8,16},{16,24},{24,0},{1,9},{9,17},{17,25},{25,1},{2,10},{10... | collective-permute-start | bytes 24584 | tf_op jit(solution)/shard_map/ppermute | solution.py:18
  89.0 3.0 %collective-permute-start.13 = (f32[2,2,512]{2,1,0:T(2,128)S(1)}, f32[2,2,512]{2,1,0:T(2,128)S(1)}, u32[]{:S(2)}, u32[]{:S(2)}) collective-permute-start(f32[2,2,512]{2,1,0:T(2,128)S(1)} %get-tuple-element.61), channel_id=1, source_target_pairs={{8,0},{16,8},{24,16},{0,24},{9,1},{17,9},{25,17},{1,25},{10,2},{18... | collective-permute-start | bytes 24584 | tf_op jit(solution)/shard_map/ppermute | solution.py:20
  92.1 9.1 %collective-permute-start.14 = (f32[2,132,2]{2,1,0:T(8,128)S(1)}, f32[2,132,2]{2,1,0:T(8,128)S(1)}, u32[]{:S(2)}, u32[]{:S(2)}) collective-permute-start(f32[2,132,2]{2,1,0:T(8,128)S(1)} %get-tuple-element.28), channel_id=1, source_target_pairs={{0,1},{1,2},{2,3},{3,4},{4,5},{5,6},{6,7},{7,0},{8,9},{9,10},{10,1... | collective-permute-start | bytes 6344 | tf_op jit(solution)/shard_map/ppermute | solution.py:18
  92.2 9.0 %collective-permute-start.15 = (f32[2,132,2]{2,1,0:T(8,128)S(1)}, f32[2,132,2]{2,1,0:T(8,128)S(1)}, u32[]{:S(2)}, u32[]{:S(2)}) collective-permute-start(f32[2,132,2]{2,1,0:T(8,128)S(1)} %get-tuple-element.29), channel_id=1, source_target_pairs={{1,0},{2,1},{3,2},{4,3},{5,4},{6,5},{7,6},{0,7},{9,8},{10,9},{11,1... | collective-permute-start | bytes 6344 | tf_op jit(solution)/shard_map/ppermute | solution.py:20
  102.5 3.1 %collective-permute-start.16 = (f32[2,2,512]{2,1,0:T(2,128)S(1)}, f32[2,2,512]{2,1,0:T(2,128)S(1)}, u32[]{:S(2)}, u32[]{:S(2)}) collective-permute-start(f32[2,2,512]{2,1,0:T(2,128)S(1)} %get-tuple-element.56), channel_id=1, source_target_pairs={{0,8},{8,16},{16,24},{24,0},{1,9},{9,17},{17,25},{25,1},{2,10},{10... | collective-permute-start | bytes 24584 | tf_op jit(solution)/shard_map/ppermute | solution.py:18
  102.9 2.7 %collective-permute-start.17 = (f32[2,2,512]{2,1,0:T(2,128)S(1)}, f32[2,2,512]{2,1,0:T(2,128)S(1)}, u32[]{:S(2)}, u32[]{:S(2)}) collective-permute-start(f32[2,2,512]{2,1,0:T(2,128)S(1)} %get-tuple-element.57), channel_id=1, source_target_pairs={{8,0},{16,8},{24,16},{0,24},{9,1},{17,9},{25,17},{1,25},{10,2},{18... | collective-permute-start | bytes 24584 | tf_op jit(solution)/shard_map/ppermute | solution.py:20
  105.8 9.0 %collective-permute-start.18 = (f32[2,132,2]{2,1,0:T(8,128)S(1)}, f32[2,132,2]{2,1,0:T(8,128)S(1)}, u32[]{:S(2)}, u32[]{:S(2)}) collective-permute-start(f32[2,132,2]{2,1,0:T(8,128)S(1)} %get-tuple-element.24), channel_id=1, source_target_pairs={{0,1},{1,2},{2,3},{3,4},{4,5},{5,6},{6,7},{7,0},{8,9},{9,10},{10,1... | collective-permute-start | bytes 6344 | tf_op jit(solution)/shard_map/ppermute | solution.py:18
  105.9 9.1 %collective-permute-start.19 = (f32[2,132,2]{2,1,0:T(8,128)S(1)}, f32[2,132,2]{2,1,0:T(8,128)S(1)}, u32[]{:S(2)}, u32[]{:S(2)}) collective-permute-start(f32[2,132,2]{2,1,0:T(8,128)S(1)} %get-tuple-element.25), channel_id=1, source_target_pairs={{1,0},{2,1},{3,2},{4,3},{5,4},{6,5},{7,6},{0,7},{9,8},{10,9},{11,1... | collective-permute-start | bytes 6344 | tf_op jit(solution)/shard_map/ppermute | solution.py:20
  116.3 3.1 %collective-permute-start.20 = (f32[2,2,512]{2,1,0:T(2,128)S(1)}, f32[2,2,512]{2,1,0:T(2,128)S(1)}, u32[]{:S(2)}, u32[]{:S(2)}) collective-permute-start(f32[2,2,512]{2,1,0:T(2,128)S(1)} %get-tuple-element.52), channel_id=1, source_target_pairs={{0,8},{8,16},{16,24},{24,0},{1,9},{9,17},{17,25},{25,1},{2,10},{10... | collective-permute-start | bytes 24584 | tf_op jit(solution)/shard_map/ppermute | solution.py:18
  116.9 2.6 %collective-permute-start.21 = (f32[2,2,512]{2,1,0:T(2,128)S(1)}, f32[2,2,512]{2,1,0:T(2,128)S(1)}, u32[]{:S(2)}, u32[]{:S(2)}) collective-permute-start(f32[2,2,512]{2,1,0:T(2,128)S(1)} %get-tuple-element.53), channel_id=1, source_target_pairs={{8,0},{16,8},{24,16},{0,24},{9,1},{17,9},{25,17},{1,25},{10,2},{18... | collective-permute-start | bytes 24584 | tf_op jit(solution)/shard_map/ppermute | solution.py:20
  119.6 9.4 %collective-permute-start.22 = (f32[2,132,2]{2,1,0:T(8,128)S(1)}, f32[2,132,2]{2,1,0:T(8,128)S(1)}, u32[]{:S(2)}, u32[]{:S(2)}) collective-permute-start(f32[2,132,2]{2,1,0:T(8,128)S(1)} %get-tuple-element.20), channel_id=1, source_target_pairs={{0,1},{1,2},{2,3},{3,4},{4,5},{5,6},{6,7},{7,0},{8,9},{9,10},{10,1... | collective-permute-start | bytes 6344 | tf_op jit(solution)/shard_map/ppermute | solution.py:18
  119.7 10.2 %collective-permute-start.23 = (f32[2,132,2]{2,1,0:T(8,128)S(1)}, f32[2,132,2]{2,1,0:T(8,128)S(1)}, u32[]{:S(2)}, u32[]{:S(2)}) collective-permute-start(f32[2,132,2]{2,1,0:T(8,128)S(1)} %get-tuple-element.21), channel_id=1, source_target_pairs={{1,0},{2,1},{3,2},{4,3},{5,4},{6,5},{7,6},{0,7},{9,8},{10,9},{11,1... | collective-permute-start | bytes 6344 | tf_op jit(solution)/shard_map/ppermute | solution.py:20
  131.2 3.1 %collective-permute-start.24 = (f32[2,2,512]{2,1,0:T(2,128)S(1)}, f32[2,2,512]{2,1,0:T(2,128)S(1)}, u32[]{:S(2)}, u32[]{:S(2)}) collective-permute-start(f32[2,2,512]{2,1,0:T(2,128)S(1)} %get-tuple-element.48), channel_id=1, source_target_pairs={{0,8},{8,16},{16,24},{24,0},{1,9},{9,17},{17,25},{25,1},{2,10},{10... | collective-permute-start | bytes 24584 | tf_op jit(solution)/shard_map/ppermute | solution.py:18
  131.4 3.0 %collective-permute-start.25 = (f32[2,2,512]{2,1,0:T(2,128)S(1)}, f32[2,2,512]{2,1,0:T(2,128)S(1)}, u32[]{:S(2)}, u32[]{:S(2)}) collective-permute-start(f32[2,2,512]{2,1,0:T(2,128)S(1)} %get-tuple-element.49), channel_id=1, source_target_pairs={{8,0},{16,8},{24,16},{0,24},{9,1},{17,9},{25,17},{1,25},{10,2},{18... | collective-permute-start | bytes 24584 | tf_op jit(solution)/shard_map/ppermute | solution.py:20
  134.5 9.0 %collective-permute-start.26 = (f32[2,132,2]{2,1,0:T(8,128)S(1)}, f32[2,132,2]{2,1,0:T(8,128)S(1)}, u32[]{:S(2)}, u32[]{:S(2)}) collective-permute-start(f32[2,132,2]{2,1,0:T(8,128)S(1)} %get-tuple-element.16), channel_id=1, source_target_pairs={{0,1},{1,2},{2,3},{3,4},{4,5},{5,6},{6,7},{7,0},{8,9},{9,10},{10,1... | collective-permute-start | bytes 6344 | tf_op jit(solution)/shard_map/ppermute | solution.py:18
  134.7 10.2 %collective-permute-start.27 = (f32[2,132,2]{2,1,0:T(8,128)S(1)}, f32[2,132,2]{2,1,0:T(8,128)S(1)}, u32[]{:S(2)}, u32[]{:S(2)}) collective-permute-start(f32[2,132,2]{2,1,0:T(8,128)S(1)} %get-tuple-element.17), channel_id=1, source_target_pairs={{1,0},{2,1},{3,2},{4,3},{5,4},{6,5},{7,6},{0,7},{9,8},{10,9},{11,1... | collective-permute-start | bytes 6344 | tf_op jit(solution)/shard_map/ppermute | solution.py:20
  146.3 3.1 %collective-permute-start.28 = (f32[2,2,512]{2,1,0:T(2,128)S(1)}, f32[2,2,512]{2,1,0:T(2,128)S(1)}, u32[]{:S(2)}, u32[]{:S(2)}) collective-permute-start(f32[2,2,512]{2,1,0:T(2,128)S(1)} %get-tuple-element.44), channel_id=1, source_target_pairs={{0,8},{8,16},{16,24},{24,0},{1,9},{9,17},{17,25},{25,1},{2,10},{10... | collective-permute-start | bytes 24584 | tf_op jit(solution)/shard_map/ppermute | solution.py:18
  146.5 3.0 %collective-permute-start.29 = (f32[2,2,512]{2,1,0:T(2,128)S(1)}, f32[2,2,512]{2,1,0:T(2,128)S(1)}, u32[]{:S(2)}, u32[]{:S(2)}) collective-permute-start(f32[2,2,512]{2,1,0:T(2,128)S(1)} %get-tuple-element.45), channel_id=1, source_target_pairs={{8,0},{16,8},{24,16},{0,24},{9,1},{17,9},{25,17},{1,25},{10,2},{18... | collective-permute-start | bytes 24584 | tf_op jit(solution)/shard_map/ppermute | solution.py:20
  149.6 9.0 %collective-permute-start.30 = (f32[2,132,2]{2,1,0:T(8,128)S(1)}, f32[2,132,2]{2,1,0:T(8,128)S(1)}, u32[]{:S(2)}, u32[]{:S(2)}) collective-permute-start(f32[2,132,2]{2,1,0:T(8,128)S(1)} %get-tuple-element.12), channel_id=1, source_target_pairs={{0,1},{1,2},{2,3},{3,4},{4,5},{5,6},{6,7},{7,0},{8,9},{9,10},{10,1... | collective-permute-start | bytes 6344 | tf_op jit(solution)/shard_map/ppermute | solution.py:18
  149.8 10.2 %collective-permute-start.31 = (f32[2,132,2]{2,1,0:T(8,128)S(1)}, f32[2,132,2]{2,1,0:T(8,128)S(1)}, u32[]{:S(2)}, u32[]{:S(2)}) collective-permute-start(f32[2,132,2]{2,1,0:T(8,128)S(1)} %get-tuple-element.13), channel_id=1, source_target_pairs={{1,0},{2,1},{3,2},{4,3},{5,4},{6,5},{7,6},{0,7},{9,8},{10,9},{11,1... | collective-permute-start | bytes 6344 | tf_op jit(solution)/shard_map/ppermute | solution.py:20
where the time goes:
time: 163 us; the launch traced here: 162 us
  starting transfers between devices  60.8 us (37%)
  waiting for transfers between devices  57.7 us (35%)
  local copies, waits for them, and re-layouts  31.8 us (20%)
  other arithmetic  11.7 us (7%)
    ppermute x16, waiting for transfers between devices, with_halo(): lax.ppermute(tail, axis, [(i, (i + 1) % count) for i in range(count)])  50.1 us
    ppermute x16, starting transfers between devices, with_halo(): lax.ppermute(head, axis, [((i + 1) % count, i) for i in range(count)])  46.3 us
    unnamed x6, local copies, waits for them, and re-layouts  24.5 us
    ppermute x16, waiting for transfers between devices, with_halo(): lax.ppermute(head, axis, [((i + 1) % count, i) for i in range(count)])  7.54 us
    ppermute x16, starting transfers between devices, with_halo(): lax.ppermute(tail, axis, [(i, (i + 1) % count) for i in range(count)])  7.29 us
    all_to_all x1, starting transfers between devices, local(): lax.all_to_all(index_panels, 'col', split_axis=2, concat_axis=1, tiled=True)  7.28 us
    all_to_all x1, local copies, waits for them, and re-layouts, local(): lax.all_to_all(index_panels, 'col', split_axis=2, concat_axis=1, tiled=True)  6.41 us
    add x8, other arithmetic, slope(): diffraction * laplace(padded)  4.96 us
  transfers between devices with their start and end apart: 33, of which 22 were waited for; matrix products, arithmetic and copies ran while one was open for 1% of the time, Pallas kernels for 0%

commit v1 on v0

--- a/solution.py
+++ b/solution.py
@@ -47,7 +47,14 @@
 
 
 def local(optical_field, index_panels):
-    planes_all = lax.all_to_all(index_panels, "col", split_axis=2, concat_axis=1, tiled=True)
+
+    def _load_sites(buf, comm_axis, d_out, on_dim):
+        o_now = lax.axis_size(comm_axis)
+        shaped = jnp.split(buf, o_now, axis=d_out)
+        y2 = lax.all_to_all(jnp.stack(shaped), comm_axis, split_axis=0, concat_axis=0)
+        return jnp.concatenate(y2, axis=on_dim)
+
+    planes_all = _load_sites(index_panels, "col", 2, 1)
     field = optical_field
     planes = None
     for step_index in range(STEPS):

time: 163 us -> 144 us (0.88)
  local copies, waits for them, and re-layouts: 31.8 us -> 12.3 us
    unnamed x6 -> x10, local copies, waits for them, and re-layouts: 24.5 us -> 10.7 us
    all_to_all x1 -> x0, local copies, waits for them, and re-layouts: 6.41 us -> none  [local(): lax.all_to_all(index_panels, 'col', split_axis=2, concat_axis=1, tiled=True)]
  transfers between devices with their start and end apart: 33 -> 33, of which waited for: 22 -> 22; matrix products, arithmetic and copies ran while one was open for 1% -> 0% of each run, Pallas kernels for 0% -> 0%
where the time goes in v1:
time: 144 us
  starting transfers between devices  60.1 us (42%)
  waiting for transfers between devices  59 us (41%)
  local copies, waits for them, and re-layouts  12.3 us (9%)
  other arithmetic  11.7 us (8%)
    ppermute x16, waiting for transfers between devices, with_halo(): lax.ppermute(tail, axis, [(i, (i + 1) % count) for i in range(count)])  50.8 us
    ppermute x16, starting transfers between devices, with_halo(): lax.ppermute(head, axis, [((i + 1) % count, i) for i in range(count)])  45.8 us
    unnamed x10, local copies, waits for them, and re-layouts  10.7 us
    ppermute x16, waiting for transfers between devices, with_halo(): lax.ppermute(head, axis, [((i + 1) % count, i) for i in range(count)])  8.25 us
    all_to_all x1, starting transfers between devices, _load_sites(): lax.all_to_all(jnp.stack(shaped), comm_axis, split_axis=0, concat_axis=0)  7.41 us
    ppermute x16, starting transfers between devices, with_halo(): lax.ppermute(tail, axis, [(i, (i + 1) % count) for i in range(count)])  6.97 us
    add x8, other arithmetic, slope(): diffraction * laplace(padded)  4.96 us
  transfers between devices with their start and end apart: 33, of which 22 were waited for; matrix products, arithmetic and copies ran while one was open for 0% of the time, Pallas kernels for 0%

profile of v1, /device:TPU:0, one launch (start us, length us, event | category | flops | bytes accessed | tf_op | source)
XLA Modules:
  0.0 143.6 jit_solution(13973525090332238260)
XLA Ops:
  0.0 1.5 %bitcast_dynamic-update-slice_fusion.7 = bf16[8,5,16,512]{3,2,1,0:T(8,128)(2,1)} fusion(bf16[5,16,4096]{2,1,0:T(8,128)(2,1)} %param.3), kind=kLoop, calls=%fused_computation.234 | loop fusion | bytes 163840
  1.5 1.5 %bitcast_dynamic-update-slice_fusion.6 = bf16[8,5,16,512]{3,2,1,0:T(8,128)(2,1)} fusion(bf16[8,5,16,512]{3,2,1,0:T(8,128)(2,1)} %bitcast_dynamic-update-slice_fusion.7, bf16[5,16,4096]{2,1,0:T(8,128)(2,1)} %param.3), kind=kLoop, calls=%fused_computation.233 | loop fusion | bytes 163840
  3.0 1.5 %bitcast_dynamic-update-slice_fusion.5 = bf16[8,5,16,512]{3,2,1,0:T(8,128)(2,1)} fusion(bf16[8,5,16,512]{3,2,1,0:T(8,128)(2,1)} %bitcast_dynamic-update-slice_fusion.6, bf16[5,16,4096]{2,1,0:T(8,128)(2,1)} %param.3), kind=kLoop, calls=%fused_computation.232 | loop fusion | bytes 163840
  4.6 1.5 %bitcast_dynamic-update-slice_fusion.4 = bf16[8,5,16,512]{3,2,1,0:T(8,128)(2,1)} fusion(bf16[8,5,16,512]{3,2,1,0:T(8,128)(2,1)} %bitcast_dynamic-update-slice_fusion.5, bf16[5,16,4096]{2,1,0:T(8,128)(2,1)} %param.3), kind=kLoop, calls=%fused_computation.231 | loop fusion | bytes 163840
  6.1 1.5 %bitcast_dynamic-update-slice_fusion.3 = bf16[8,5,16,512]{3,2,1,0:T(8,128)(2,1)} fusion(bf16[8,5,16,512]{3,2,1,0:T(8,128)(2,1)} %bitcast_dynamic-update-slice_fusion.4, bf16[5,16,4096]{2,1,0:T(8,128)(2,1)} %param.3), kind=kLoop, calls=%fused_computation.230 | loop fusion | bytes 163840
  7.6 1.5 %bitcast_dynamic-update-slice_fusion.2 = bf16[8,5,16,512]{3,2,1,0:T(8,128)(2,1)} fusion(bf16[8,5,16,512]{3,2,1,0:T(8,128)(2,1)} %bitcast_dynamic-update-slice_fusion.3, bf16[5,16,4096]{2,1,0:T(8,128)(2,1)} %param.3), kind=kLoop, calls=%fused_computation.229 | loop fusion | bytes 163840
  9.1 1.5 %bitcast_dynamic-update-slice_fusion.1 = bf16[8,5,16,512]{3,2,1,0:T(8,128)(2,1)} fusion(bf16[8,5,16,512]{3,2,1,0:T(8,128)(2,1)} %bitcast_dynamic-update-slice_fusion.2, bf16[5,16,4096]{2,1,0:T(8,128)(2,1)} %param.3), kind=kLoop, calls=%fused_computation.228 | loop fusion | bytes 163840
  10.6 1.5 %bitcast_dynamic-update-slice_fusion = bf16[8,5,16,512]{3,2,1,0:T(8,128)(2,1)} fusion(bf16[8,5,16,512]{3,2,1,0:T(8,128)(2,1)} %bitcast_dynamic-update-slice_fusion.1, bf16[5,16,4096]{2,1,0:T(8,128)(2,1)} %param.3), kind=kLoop, calls=%fused_computation.227 | loop fusion | bytes 163840 | tf_op jit(solution)/shard_map/stack | solution.py:54
  12.2 7.4 %all-to-all-start = ((bf16[8,5,16,512]{3,2,1,0:T(8,128)(2,1)}), bf16[8,5,16,512]{3,2,1,0:T(8,128)(2,1)S(1)}, u32[]{:S(2)}, u32[]{:S(2)}) async-start(bf16[8,5,16,512]{3,2,1,0:T(8,128)(2,1)} %bitcast_dynamic-update-slice_fusion), calls=%async_computation | async-start | bytes 1310720 | tf_op jit(solution)/shard_map/all_to_all | solution.py:54
  19.6 0.7 collective-permute-start.1
  20.3 1.3 collective-permute-done.1
  21.7 1.7 %collective-permute-done = f32[2,2,512]{2,1,0:T(2,128)S(1)} collective-permute-done((f32[2,2,512]{2,1,0:T(2,128)S(1)}, f32[2,2,512]{2,1,0:T(2,128)S(1)}, u32[]{:S(2)}, u32[]{:S(2)}) %collective-permute-start) | collective-permute-done | bytes 8224 | tf_op jit(solution)/shard_map/ppermute | solution.py:18
  23.5 1.8 %collective-permute-start.2 = (f32[2,132,2]{2,1,0:T(8,128)S(1)}, f32[2,132,2]{2,1,0:T(8,128)S(1)}, u32[]{:S(2)}, u32[]{:S(2)}) collective-permute-start(f32[2,132,2]{2,1,0:T(8,128)S(1)} %get-tuple-element.40), channel_id=1, source_target_pairs={{0,1},{1,2},{2,3},{3,4},{4,5},{5,6},{6,7},{7,0},{8,9},{9,10},{10,1... | collective-permute-start | bytes 6344 | tf_op jit(solution)/shard_map/ppermute | solution.py:18
  25.3 3.0 %collective-permute-start.3 = (f32[2,132,2]{2,1,0:T(8,128)S(1)}, f32[2,132,2]{2,1,0:T(8,128)S(1)}, u32[]{:S(2)}, u32[]{:S(2)}) collective-permute-start(f32[2,132,2]{2,1,0:T(8,128)S(1)} %get-tuple-element.41), channel_id=1, source_target_pairs={{1,0},{2,1},{3,2},{4,3},{5,4},{6,5},{7,6},{0,7},{9,8},{10,9},{11,1... | collective-permute-start | bytes 6344 | tf_op jit(solution)/shard_map/ppermute | solution.py:20
  28.3 10.0 %collective-permute-done.2 = f32[2,132,2]{2,1,0:T(8,128)S(1)} collective-permute-done((f32[2,132,2]{2,1,0:T(8,128)S(1)}, f32[2,132,2]{2,1,0:T(8,128)S(1)}, u32[]{:S(2)}, u32[]{:S(2)}) %collective-permute-start.2) | collective-permute-done | bytes 2144 | tf_op jit(solution)/shard_map/ppermute | solution.py:18
  39.6 1.7 %collective-permute-start.5 = (f32[2,2,512]{2,1,0:T(2,128)S(1)}, f32[2,2,512]{2,1,0:T(2,128)S(1)}, u32[]{:S(2)}, u32[]{:S(2)}) collective-permute-start(f32[2,2,512]{2,1,0:T(2,128)S(1)} %get-tuple-element.69), channel_id=1, source_target_pairs={{8,0},{16,8},{24,16},{0,24},{9,1},{17,9},{25,17},{1,25},{10,2},{18... | collective-permute-start | bytes 24584 | tf_op jit(solution)/shard_map/ppermute | solution.py:20
  41.3 1.3 collective-permute-done.4
  42.8 2.8 %collective-permute-start.6 = (f32[2,132,2]{2,1,0:T(8,128)S(1)}, f32[2,132,2]{2,1,0:T(8,128)S(1)}, u32[]{:S(2)}, u32[]{:S(2)}) collective-permute-start(f32[2,132,2]{2,1,0:T(8,128)S(1)} %get-tuple-element.36), channel_id=1, source_target_pairs={{0,1},{1,2},{2,3},{3,4},{4,5},{5,6},{6,7},{7,0},{8,9},{9,10},{10,1... | collective-permute-start | bytes 6344 | tf_op jit(solution)/shard_map/ppermute | solution.py:18
  45.6 2.0 %collective-permute-start.7 = (f32[2,132,2]{2,1,0:T(8,128)S(1)}, f32[2,132,2]{2,1,0:T(8,128)S(1)}, u32[]{:S(2)}, u32[]{:S(2)}) collective-permute-start(f32[2,132,2]{2,1,0:T(8,128)S(1)} %get-tuple-element.37), channel_id=1, source_target_pairs={{1,0},{2,1},{3,2},{4,3},{5,4},{6,5},{7,6},{0,7},{9,8},{10,9},{11,1... | collective-permute-start | bytes 6344 | tf_op jit(solution)/shard_map/ppermute | solution.py:20
  47.6 4.6 %collective-permute-done.6 = f32[2,132,2]{2,1,0:T(8,128)S(1)} collective-permute-done((f32[2,132,2]{2,1,0:T(8,128)S(1)}, f32[2,132,2]{2,1,0:T(8,128)S(1)}, u32[]{:S(2)}, u32[]{:S(2)}) %collective-permute-start.6) | collective-permute-done | bytes 2144 | tf_op jit(solution)/shard_map/ppermute | solution.py:18
  52.1 2.9 %collective-permute-done.7 = f32[2,132,2]{2,1,0:T(8,128)S(1)} collective-permute-done((f32[2,132,2]{2,1,0:T(8,128)S(1)}, f32[2,132,2]{2,1,0:T(8,128)S(1)}, u32[]{:S(2)}, u32[]{:S(2)}) %collective-permute-start.7) | collective-permute-done | bytes 2144 | tf_op jit(solution)/shard_map/ppermute | solution.py:20
  56.3 1.6 %collective-permute-start.9 = (f32[2,2,512]{2,1,0:T(2,128)S(1)}, f32[2,2,512]{2,1,0:T(2,128)S(1)}, u32[]{:S(2)}, u32[]{:S(2)}) collective-permute-start(f32[2,2,512]{2,1,0:T(2,128)S(1)} %get-tuple-element.65), channel_id=1, source_target_pairs={{8,0},{16,8},{24,16},{0,24},{9,1},{17,9},{25,17},{1,25},{10,2},{18... | collective-permute-start | bytes 24584 | tf_op jit(solution)/shard_map/ppermute | solution.py:20
  57.9 1.3 collective-permute-done.8
  59.5 4.7 %collective-permute-start.11 = (f32[2,132,2]{2,1,0:T(8,128)S(1)}, f32[2,132,2]{2,1,0:T(8,128)S(1)}, u32[]{:S(2)}, u32[]{:S(2)}) collective-permute-start(f32[2,132,2]{2,1,0:T(8,128)S(1)} %get-tuple-element.33), channel_id=1, source_target_pairs={{1,0},{2,1},{3,2},{4,3},{5,4},{6,5},{7,6},{0,7},{9,8},{10,9},{11,1... | collective-permute-start | bytes 6344 | tf_op jit(solution)/shard_map/ppermute | solution.py:20
  64.2 4.6 %collective-permute-done.10 = f32[2,132,2]{2,1,0:T(8,128)S(1)} collective-permute-done((f32[2,132,2]{2,1,0:T(8,128)S(1)}, f32[2,132,2]{2,1,0:T(8,128)S(1)}, u32[]{:S(2)}, u32[]{:S(2)}) %collective-permute-start.10) | collective-permute-done | bytes 2144 | tf_op jit(solution)/shard_map/ppermute | solution.py:18
  70.3 1.6 %collective-permute-start.13 = (f32[2,2,512]{2,1,0:T(2,128)S(1)}, f32[2,2,512]{2,1,0:T(2,128)S(1)}, u32[]{:S(2)}, u32[]{:S(2)}) collective-permute-start(f32[2,2,512]{2,1,0:T(2,128)S(1)} %get-tuple-element.61), channel_id=1, source_target_pairs={{8,0},{16,8},{24,16},{0,24},{9,1},{17,9},{25,17},{1,25},{10,2},{18... | collective-permute-start | bytes 24584 | tf_op jit(solution)/shard_map/ppermute | solution.py:20
  71.9 1.3 collective-permute-done.12
  73.4 4.7 %collective-permute-start.15 = (f32[2,132,2]{2,1,0:T(8,128)S(1)}, f32[2,132,2]{2,1,0:T(8,128)S(1)}, u32[]{:S(2)}, u32[]{:S(2)}) collective-permute-start(f32[2,132,2]{2,1,0:T(8,128)S(1)} %get-tuple-element.29), channel_id=1, source_target_pairs={{1,0},{2,1},{3,2},{4,3},{5,4},{6,5},{7,6},{0,7},{9,8},{10,9},{11,1... | collective-permute-start | bytes 6344 | tf_op jit(solution)/shard_map/ppermute | solution.py:20
  78.2 4.3 %collective-permute-done.14 = f32[2,132,2]{2,1,0:T(8,128)S(1)} collective-permute-done((f32[2,132,2]{2,1,0:T(8,128)S(1)}, f32[2,132,2]{2,1,0:T(8,128)S(1)}, u32[]{:S(2)}, u32[]{:S(2)}) %collective-permute-start.14) | collective-permute-done | bytes 2144 | tf_op jit(solution)/shard_map/ppermute | solution.py:18
  84.2 1.4 collective-permute-start.17
  85.6 1.3 collective-permute-done.16
  87.1 5.0 %collective-permute-start.19 = (f32[2,132,2]{2,1,0:T(8,128)S(1)}, f32[2,132,2]{2,1,0:T(8,128)S(1)}, u32[]{:S(2)}, u32[]{:S(2)}) collective-permute-start(f32[2,132,2]{2,1,0:T(8,128)S(1)} %get-tuple-element.25), channel_id=1, source_target_pairs={{1,0},{2,1},{3,2},{4,3},{5,4},{6,5},{7,6},{0,7},{9,8},{10,9},{11,1... | collective-permute-start | bytes 6344 | tf_op jit(solution)/shard_map/ppermute | solution.py:20
  92.1 4.0 %collective-permute-done.18 = f32[2,132,2]{2,1,0:T(8,128)S(1)} collective-permute-done((f32[2,132,2]{2,1,0:T(8,128)S(1)}, f32[2,132,2]{2,1,0:T(8,128)S(1)}, u32[]{:S(2)}, u32[]{:S(2)}) %collective-permute-start.18) | collective-permute-done | bytes 2144 | tf_op jit(solution)/shard_map/ppermute | solution.py:18
  97.9 1.3 collective-permute-start.21
  99.2 1.3 collective-permute-done.20
  100.8 5.5 %collective-permute-start.23 = (f32[2,132,2]{2,1,0:T(8,128)S(1)}, f32[2,132,2]{2,1,0:T(8,128)S(1)}, u32[]{:S(2)}, u32[]{:S(2)}) collective-permute-start(f32[2,132,2]{2,1,0:T(8,128)S(1)} %get-tuple-element.21), channel_id=1, source_target_pairs={{1,0},{2,1},{3,2},{4,3},{5,4},{6,5},{7,6},{0,7},{9,8},{10,9},{11,1... | collective-permute-start | bytes 6344 | tf_op jit(solution)/shard_map/ppermute | solution.py:20
  106.3 4.3 %collective-permute-done.22 = f32[2,132,2]{2,1,0:T(8,128)S(1)} collective-permute-done((f32[2,132,2]{2,1,0:T(8,128)S(1)}, f32[2,132,2]{2,1,0:T(8,128)S(1)}, u32[]{:S(2)}, u32[]{:S(2)}) %collective-permute-start.22) | collective-permute-done | bytes 2144 | tf_op jit(solution)/shard_map/ppermute | solution.py:18
  112.6 1.6 %collective-permute-start.25 = (f32[2,2,512]{2,1,0:T(2,128)S(1)}, f32[2,2,512]{2,1,0:T(2,128)S(1)}, u32[]{:S(2)}, u32[]{:S(2)}) collective-permute-start(f32[2,2,512]{2,1,0:T(2,128)S(1)} %get-tuple-element.49), channel_id=1, source_target_pairs={{8,0},{16,8},{24,16},{0,24},{9,1},{17,9},{25,17},{1,25},{10,2},{18... | collective-permute-start | bytes 24584 | tf_op jit(solution)/shard_map/ppermute | solution.py:20
  114.2 1.3 collective-permute-done.24
  115.9 4.8 %collective-permute-start.27 = (f32[2,132,2]{2,1,0:T(8,128)S(1)}, f32[2,132,2]{2,1,0:T(8,128)S(1)}, u32[]{:S(2)}, u32[]{:S(2)}) collective-permute-start(f32[2,132,2]{2,1,0:T(8,128)S(1)} %get-tuple-element.17), channel_id=1, source_target_pairs={{1,0},{2,1},{3,2},{4,3},{5,4},{6,5},{7,6},{0,7},{9,8},{10,9},{11,1... | collective-permute-start | bytes 6344 | tf_op jit(solution)/shard_map/ppermute | solution.py:20
  120.7 4.0 %collective-permute-done.26 = f32[2,132,2]{2,1,0:T(8,128)S(1)} collective-permute-done((f32[2,132,2]{2,1,0:T(8,128)S(1)}, f32[2,132,2]{2,1,0:T(8,128)S(1)}, u32[]{:S(2)}, u32[]{:S(2)}) %collective-permute-start.26) | collective-permute-done | bytes 2144 | tf_op jit(solution)/shard_map/ppermute | solution.py:18
  124.6 1.5 %collective-permute-done.27 = f32[2,132,2]{2,1,0:T(8,128)S(1)} collective-permute-done((f32[2,132,2]{2,1,0:T(8,128)S(1)}, f32[2,132,2]{2,1,0:T(8,128)S(1)}, u32[]{:S(2)}, u32[]{:S(2)}) %collective-permute-start.27) | collective-permute-done | bytes 2144 | tf_op jit(solution)/shard_map/ppermute | solution.py:20
  127.7 1.6 %collective-permute-start.29 = (f32[2,2,512]{2,1,0:T(2,128)S(1)}, f32[2,2,512]{2,1,0:T(2,128)S(1)}, u32[]{:S(2)}, u32[]{:S(2)}) collective-permute-start(f32[2,2,512]{2,1,0:T(2,128)S(1)} %get-tuple-element.45), channel_id=1, source_target_pairs={{8,0},{16,8},{24,16},{0,24},{9,1},{17,9},{25,17},{1,25},{10,2},{18... | collective-permute-start | bytes 24584 | tf_op jit(solution)/shard_map/ppermute | solution.py:20
  129.3 1.3 collective-permute-done.28
  131.0 4.5 %collective-permute-start.31 = (f32[2,132,2]{2,1,0:T(8,128)S(1)}, f32[2,132,2]{2,1,0:T(8,128)S(1)}, u32[]{:S(2)}, u32[]{:S(2)}) collective-permute-start(f32[2,132,2]{2,1,0:T(8,128)S(1)} %get-tuple-element.13), channel_id=1, source_target_pairs={{1,0},{2,1},{3,2},{4,3},{5,4},{6,5},{7,6},{0,7},{9,8},{10,9},{11,1... | collective-permute-start | bytes 6344 | tf_op jit(solution)/shard_map/ppermute | solution.py:20
  135.6 4.2 %collective-permute-done.30 = f32[2,132,2]{2,1,0:T(8,128)S(1)} collective-permute-done((f32[2,132,2]{2,1,0:T(8,128)S(1)}, f32[2,132,2]{2,1,0:T(8,128)S(1)}, u32[]{:S(2)}, u32[]{:S(2)}) %collective-permute-start.30) | collective-permute-done | bytes 2144 | tf_op jit(solution)/shard_map/ppermute | solution.py:18
  139.7 1.5 %collective-permute-done.31 = f32[2,132,2]{2,1,0:T(8,128)S(1)} collective-permute-done((f32[2,132,2]{2,1,0:T(8,128)S(1)}, f32[2,132,2]{2,1,0:T(8,128)S(1)}, u32[]{:S(2)}, u32[]{:S(2)}) %collective-permute-start.31) | collective-permute-done | bytes 2144 | tf_op jit(solution)/shard_map/ppermute | solution.py:20
  142.2 1.4 fusion.97
  (79 shorter events, 13.9 us)
Async XLA Ops:
  12.2 7.4 %copy-start = (f32[2,128,512]{2,1,0:T(8,128)S(1)}, f32[2,128,512]{2,1,0:T(8,128)}, u32[]{:S(2)}) copy-start(f32[2,128,512]{2,1,0:T(8,128)} %param.2) | copy-start | bytes 1572868
  12.2 26.4 %all-to-all-start = ((bf16[8,5,16,512]{3,2,1,0:T(8,128)(2,1)}), bf16[8,5,16,512]{3,2,1,0:T(8,128)(2,1)S(1)}, u32[]{:S(2)}, u32[]{:S(2)}) async-start(bf16[8,5,16,512]{3,2,1,0:T(8,128)(2,1)} %bitcast_dynamic-update-slice_fusion), calls=%async_computation | async-start | bytes 1310720 | tf_op jit(solution)/shard_map/all_to_all | solution.py:54
  19.6 2.1 %collective-permute-start.1 = (f32[2,2,512]{2,1,0:T(2,128)S(1)}, f32[2,2,512]{2,1,0:T(2,128)S(1)}, u32[]{:S(2)}, u32[]{:S(2)}) collective-permute-start(f32[2,2,512]{2,1,0:T(2,128)S(1)} %get-tuple-element.72), channel_id=1, source_target_pairs={{8,0},{16,8},{24,16},{0,24},{9,1},{17,9},{25,17},{1,25},{10,2},{18... | collective-permute-start | bytes 24584 | tf_op jit(solution)/shard_map/ppermute | solution.py:20
  20.3 3.1 %collective-permute-start = (f32[2,2,512]{2,1,0:T(2,128)S(1)}, f32[2,2,512]{2,1,0:T(2,128)S(1)}, u32[]{:S(2)}, u32[]{:S(2)}) collective-permute-start(f32[2,2,512]{2,1,0:T(2,128)S(1)} %get-tuple-element.73), channel_id=1, source_target_pairs={{0,8},{8,16},{16,24},{24,0},{1,9},{9,17},{17,25},{25,1},{2,10},{10... | collective-permute-start | bytes 24584 | tf_op jit(solution)/shard_map/ppermute | solution.py:18
  23.5 14.7 %collective-permute-start.2 = (f32[2,132,2]{2,1,0:T(8,128)S(1)}, f32[2,132,2]{2,1,0:T(8,128)S(1)}, u32[]{:S(2)}, u32[]{:S(2)}) collective-permute-start(f32[2,132,2]{2,1,0:T(8,128)S(1)} %get-tuple-element.40), channel_id=1, source_target_pairs={{0,1},{1,2},{2,3},{3,4},{4,5},{5,6},{6,7},{7,0},{8,9},{9,10},{10,1... | collective-permute-start | bytes 6344 | tf_op jit(solution)/shard_map/ppermute | solution.py:18
  25.3 13.0 %collective-permute-start.3 = (f32[2,132,2]{2,1,0:T(8,128)S(1)}, f32[2,132,2]{2,1,0:T(8,128)S(1)}, u32[]{:S(2)}, u32[]{:S(2)}) collective-permute-start(f32[2,132,2]{2,1,0:T(8,128)S(1)} %get-tuple-element.41), channel_id=1, source_target_pairs={{1,0},{2,1},{3,2},{4,3},{5,4},{6,5},{7,6},{0,7},{9,8},{10,9},{11,1... | collective-permute-start | bytes 6344 | tf_op jit(solution)/shard_map/ppermute | solution.py:20
  39.5 3.1 %collective-permute-start.4 = (f32[2,2,512]{2,1,0:T(2,128)S(1)}, f32[2,2,512]{2,1,0:T(2,128)S(1)}, u32[]{:S(2)}, u32[]{:S(2)}) collective-permute-start(f32[2,2,512]{2,1,0:T(2,128)S(1)} %get-tuple-element.68), channel_id=1, source_target_pairs={{0,8},{8,16},{16,24},{24,0},{1,9},{9,17},{17,25},{25,1},{2,10},{10... | collective-permute-start | bytes 24584 | tf_op jit(solution)/shard_map/ppermute | solution.py:18
  39.6 3.1 %collective-permute-start.5 = (f32[2,2,512]{2,1,0:T(2,128)S(1)}, f32[2,2,512]{2,1,0:T(2,128)S(1)}, u32[]{:S(2)}, u32[]{:S(2)}) collective-permute-start(f32[2,2,512]{2,1,0:T(2,128)S(1)} %get-tuple-element.69), channel_id=1, source_target_pairs={{8,0},{16,8},{24,16},{0,24},{9,1},{17,9},{25,17},{1,25},{10,2},{18... | collective-permute-start | bytes 24584 | tf_op jit(solution)/shard_map/ppermute | solution.py:20
  42.8 9.3 %collective-permute-start.6 = (f32[2,132,2]{2,1,0:T(8,128)S(1)}, f32[2,132,2]{2,1,0:T(8,128)S(1)}, u32[]{:S(2)}, u32[]{:S(2)}) collective-permute-start(f32[2,132,2]{2,1,0:T(8,128)S(1)} %get-tuple-element.36), channel_id=1, source_target_pairs={{0,1},{1,2},{2,3},{3,4},{4,5},{5,6},{6,7},{7,0},{8,9},{9,10},{10,1... | collective-permute-start | bytes 6344 | tf_op jit(solution)/shard_map/ppermute | solution.py:18
  45.6 9.4 %collective-permute-start.7 = (f32[2,132,2]{2,1,0:T(8,128)S(1)}, f32[2,132,2]{2,1,0:T(8,128)S(1)}, u32[]{:S(2)}, u32[]{:S(2)}) collective-permute-start(f32[2,132,2]{2,1,0:T(8,128)S(1)} %get-tuple-element.37), channel_id=1, source_target_pairs={{1,0},{2,1},{3,2},{4,3},{5,4},{6,5},{7,6},{0,7},{9,8},{10,9},{11,1... | collective-permute-start | bytes 6344 | tf_op jit(solution)/shard_map/ppermute | solution.py:20
  56.1 3.1 %collective-permute-start.8 = (f32[2,2,512]{2,1,0:T(2,128)S(1)}, f32[2,2,512]{2,1,0:T(2,128)S(1)}, u32[]{:S(2)}, u32[]{:S(2)}) collective-permute-start(f32[2,2,512]{2,1,0:T(2,128)S(1)} %get-tuple-element.64), channel_id=1, source_target_pairs={{0,8},{8,16},{16,24},{24,0},{1,9},{9,17},{17,25},{25,1},{2,10},{10... | collective-permute-start | bytes 24584 | tf_op jit(solution)/shard_map/ppermute | solution.py:18
  56.3 3.0 %collective-permute-start.9 = (f32[2,2,512]{2,1,0:T(2,128)S(1)}, f32[2,2,512]{2,1,0:T(2,128)S(1)}, u32[]{:S(2)}, u32[]{:S(2)}) collective-permute-start(f32[2,2,512]{2,1,0:T(2,128)S(1)} %get-tuple-element.65), channel_id=1, source_target_pairs={{8,0},{16,8},{24,16},{0,24},{9,1},{17,9},{25,17},{1,25},{10,2},{18... | collective-permute-start | bytes 24584 | tf_op jit(solution)/shard_map/ppermute | solution.py:20
  59.4 9.3 %collective-permute-start.10 = (f32[2,132,2]{2,1,0:T(8,128)S(1)}, f32[2,132,2]{2,1,0:T(8,128)S(1)}, u32[]{:S(2)}, u32[]{:S(2)}) collective-permute-start(f32[2,132,2]{2,1,0:T(8,128)S(1)} %get-tuple-element.32), channel_id=1, source_target_pairs={{0,1},{1,2},{2,3},{3,4},{4,5},{5,6},{6,7},{7,0},{8,9},{9,10},{10,1... | collective-permute-start | bytes 6344 | tf_op jit(solution)/shard_map/ppermute | solution.py:18
  59.5 9.5 %collective-permute-start.11 = (f32[2,132,2]{2,1,0:T(8,128)S(1)}, f32[2,132,2]{2,1,0:T(8,128)S(1)}, u32[]{:S(2)}, u32[]{:S(2)}) collective-permute-start(f32[2,132,2]{2,1,0:T(8,128)S(1)} %get-tuple-element.33), channel_id=1, source_target_pairs={{1,0},{2,1},{3,2},{4,3},{5,4},{6,5},{7,6},{0,7},{9,8},{10,9},{11,1... | collective-permute-start | bytes 6344 | tf_op jit(solution)/shard_map/ppermute | solution.py:20
  70.1 3.1 %collective-permute-start.12 = (f32[2,2,512]{2,1,0:T(2,128)S(1)}, f32[2,2,512]{2,1,0:T(2,128)S(1)}, u32[]{:S(2)}, u32[]{:S(2)}) collective-permute-start(f32[2,2,512]{2,1,0:T(2,128)S(1)} %get-tuple-element.60), channel_id=1, source_target_pairs={{0,8},{8,16},{16,24},{24,0},{1,9},{9,17},{17,25},{25,1},{2,10},{10... | collective-permute-start | bytes 24584 | tf_op jit(solution)/shard_map/ppermute | solution.py:18
  70.3 3.0 %collective-permute-start.13 = (f32[2,2,512]{2,1,0:T(2,128)S(1)}, f32[2,2,512]{2,1,0:T(2,128)S(1)}, u32[]{:S(2)}, u32[]{:S(2)}) collective-permute-start(f32[2,2,512]{2,1,0:T(2,128)S(1)} %get-tuple-element.61), channel_id=1, source_target_pairs={{8,0},{16,8},{24,16},{0,24},{9,1},{17,9},{25,17},{1,25},{10,2},{18... | collective-permute-start | bytes 24584 | tf_op jit(solution)/shard_map/ppermute | solution.py:20
  73.4 9.1 %collective-permute-start.14 = (f32[2,132,2]{2,1,0:T(8,128)S(1)}, f32[2,132,2]{2,1,0:T(8,128)S(1)}, u32[]{:S(2)}, u32[]{:S(2)}) collective-permute-start(f32[2,132,2]{2,1,0:T(8,128)S(1)} %get-tuple-element.28), channel_id=1, source_target_pairs={{0,1},{1,2},{2,3},{3,4},{4,5},{5,6},{6,7},{7,0},{8,9},{9,10},{10,1... | collective-permute-start | bytes 6344 | tf_op jit(solution)/shard_map/ppermute | solution.py:18
  73.4 9.0 %collective-permute-start.15 = (f32[2,132,2]{2,1,0:T(8,128)S(1)}, f32[2,132,2]{2,1,0:T(8,128)S(1)}, u32[]{:S(2)}, u32[]{:S(2)}) collective-permute-start(f32[2,132,2]{2,1,0:T(8,128)S(1)} %get-tuple-element.29), channel_id=1, source_target_pairs={{1,0},{2,1},{3,2},{4,3},{5,4},{6,5},{7,6},{0,7},{9,8},{10,9},{11,1... | collective-permute-start | bytes 6344 | tf_op jit(solution)/shard_map/ppermute | solution.py:20
  83.8 3.1 %collective-permute-start.16 = (f32[2,2,512]{2,1,0:T(2,128)S(1)}, f32[2,2,512]{2,1,0:T(2,128)S(1)}, u32[]{:S(2)}, u32[]{:S(2)}) collective-permute-start(f32[2,2,512]{2,1,0:T(2,128)S(1)} %get-tuple-element.56), channel_id=1, source_target_pairs={{0,8},{8,16},{16,24},{24,0},{1,9},{9,17},{17,25},{25,1},{2,10},{10... | collective-permute-start | bytes 24584 | tf_op jit(solution)/shard_map/ppermute | solution.py:18
  84.2 2.7 %collective-permute-start.17 = (f32[2,2,512]{2,1,0:T(2,128)S(1)}, f32[2,2,512]{2,1,0:T(2,128)S(1)}, u32[]{:S(2)}, u32[]{:S(2)}) collective-permute-start(f32[2,2,512]{2,1,0:T(2,128)S(1)} %get-tuple-element.57), channel_id=1, source_target_pairs={{8,0},{16,8},{24,16},{0,24},{9,1},{17,9},{25,17},{1,25},{10,2},{18... | collective-permute-start | bytes 24584 | tf_op jit(solution)/shard_map/ppermute | solution.py:20
  87.0 9.0 %collective-permute-start.18 = (f32[2,132,2]{2,1,0:T(8,128)S(1)}, f32[2,132,2]{2,1,0:T(8,128)S(1)}, u32[]{:S(2)}, u32[]{:S(2)}) collective-permute-start(f32[2,132,2]{2,1,0:T(8,128)S(1)} %get-tuple-element.24), channel_id=1, source_target_pairs={{0,1},{1,2},{2,3},{3,4},{4,5},{5,6},{6,7},{7,0},{8,9},{9,10},{10,1... | collective-permute-start | bytes 6344 | tf_op jit(solution)/shard_map/ppermute | solution.py:18
  87.1 8.9 %collective-permute-start.19 = (f32[2,132,2]{2,1,0:T(8,128)S(1)}, f32[2,132,2]{2,1,0:T(8,128)S(1)}, u32[]{:S(2)}, u32[]{:S(2)}) collective-permute-start(f32[2,132,2]{2,1,0:T(8,128)S(1)} %get-tuple-element.25), channel_id=1, source_target_pairs={{1,0},{2,1},{3,2},{4,3},{5,4},{6,5},{7,6},{0,7},{9,8},{10,9},{11,1... | collective-permute-start | bytes 6344 | tf_op jit(solution)/shard_map/ppermute | solution.py:20
  97.4 3.1 %collective-permute-start.20 = (f32[2,2,512]{2,1,0:T(2,128)S(1)}, f32[2,2,512]{2,1,0:T(2,128)S(1)}, u32[]{:S(2)}, u32[]{:S(2)}) collective-permute-start(f32[2,2,512]{2,1,0:T(2,128)S(1)} %get-tuple-element.52), channel_id=1, source_target_pairs={{0,8},{8,16},{16,24},{24,0},{1,9},{9,17},{17,25},{25,1},{2,10},{10... | collective-permute-start | bytes 24584 | tf_op jit(solution)/shard_map/ppermute | solution.py:18
  97.9 2.7 %collective-permute-start.21 = (f32[2,2,512]{2,1,0:T(2,128)S(1)}, f32[2,2,512]{2,1,0:T(2,128)S(1)}, u32[]{:S(2)}, u32[]{:S(2)}) collective-permute-start(f32[2,2,512]{2,1,0:T(2,128)S(1)} %get-tuple-element.53), channel_id=1, source_target_pairs={{8,0},{16,8},{24,16},{0,24},{9,1},{17,9},{25,17},{1,25},{10,2},{18... | collective-permute-start | bytes 24584 | tf_op jit(solution)/shard_map/ppermute | solution.py:20
  100.7 9.9 %collective-permute-start.22 = (f32[2,132,2]{2,1,0:T(8,128)S(1)}, f32[2,132,2]{2,1,0:T(8,128)S(1)}, u32[]{:S(2)}, u32[]{:S(2)}) collective-permute-start(f32[2,132,2]{2,1,0:T(8,128)S(1)} %get-tuple-element.20), channel_id=1, source_target_pairs={{0,1},{1,2},{2,3},{3,4},{4,5},{5,6},{6,7},{7,0},{8,9},{9,10},{10,1... | collective-permute-start | bytes 6344 | tf_op jit(solution)/shard_map/ppermute | solution.py:18
  100.8 10.3 %collective-permute-start.23 = (f32[2,132,2]{2,1,0:T(8,128)S(1)}, f32[2,132,2]{2,1,0:T(8,128)S(1)}, u32[]{:S(2)}, u32[]{:S(2)}) collective-permute-start(f32[2,132,2]{2,1,0:T(8,128)S(1)} %get-tuple-element.21), channel_id=1, source_target_pairs={{1,0},{2,1},{3,2},{4,3},{5,4},{6,5},{7,6},{0,7},{9,8},{10,9},{11,1... | collective-permute-start | bytes 6344 | tf_op jit(solution)/shard_map/ppermute | solution.py:20
  112.4 3.1 %collective-permute-start.24 = (f32[2,2,512]{2,1,0:T(2,128)S(1)}, f32[2,2,512]{2,1,0:T(2,128)S(1)}, u32[]{:S(2)}, u32[]{:S(2)}) collective-permute-start(f32[2,2,512]{2,1,0:T(2,128)S(1)} %get-tuple-element.48), channel_id=1, source_target_pairs={{0,8},{8,16},{16,24},{24,0},{1,9},{9,17},{17,25},{25,1},{2,10},{10... | collective-permute-start | bytes 24584 | tf_op jit(solution)/shard_map/ppermute | solution.py:18
  112.6 3.0 %collective-permute-start.25 = (f32[2,2,512]{2,1,0:T(2,128)S(1)}, f32[2,2,512]{2,1,0:T(2,128)S(1)}, u32[]{:S(2)}, u32[]{:S(2)}) collective-permute-start(f32[2,2,512]{2,1,0:T(2,128)S(1)} %get-tuple-element.49), channel_id=1, source_target_pairs={{8,0},{16,8},{24,16},{0,24},{9,1},{17,9},{25,17},{1,25},{10,2},{18... | collective-permute-start | bytes 24584 | tf_op jit(solution)/shard_map/ppermute | solution.py:20
  115.7 9.0 %collective-permute-start.26 = (f32[2,132,2]{2,1,0:T(8,128)S(1)}, f32[2,132,2]{2,1,0:T(8,128)S(1)}, u32[]{:S(2)}, u32[]{:S(2)}) collective-permute-start(f32[2,132,2]{2,1,0:T(8,128)S(1)} %get-tuple-element.16), channel_id=1, source_target_pairs={{0,1},{1,2},{2,3},{3,4},{4,5},{5,6},{6,7},{7,0},{8,9},{9,10},{10,1... | collective-permute-start | bytes 6344 | tf_op jit(solution)/shard_map/ppermute | solution.py:18
  115.9 10.2 %collective-permute-start.27 = (f32[2,132,2]{2,1,0:T(8,128)S(1)}, f32[2,132,2]{2,1,0:T(8,128)S(1)}, u32[]{:S(2)}, u32[]{:S(2)}) collective-permute-start(f32[2,132,2]{2,1,0:T(8,128)S(1)} %get-tuple-element.17), channel_id=1, source_target_pairs={{1,0},{2,1},{3,2},{4,3},{5,4},{6,5},{7,6},{0,7},{9,8},{10,9},{11,1... | collective-permute-start | bytes 6344 | tf_op jit(solution)/shard_map/ppermute | solution.py:20
  127.5 3.1 %collective-permute-start.28 = (f32[2,2,512]{2,1,0:T(2,128)S(1)}, f32[2,2,512]{2,1,0:T(2,128)S(1)}, u32[]{:S(2)}, u32[]{:S(2)}) collective-permute-start(f32[2,2,512]{2,1,0:T(2,128)S(1)} %get-tuple-element.44), channel_id=1, source_target_pairs={{0,8},{8,16},{16,24},{24,0},{1,9},{9,17},{17,25},{25,1},{2,10},{10... | collective-permute-start | bytes 24584 | tf_op jit(solution)/shard_map/ppermute | solution.py:18
  127.7 3.0 %collective-permute-start.29 = (f32[2,2,512]{2,1,0:T(2,128)S(1)}, f32[2,2,512]{2,1,0:T(2,128)S(1)}, u32[]{:S(2)}, u32[]{:S(2)}) collective-permute-start(f32[2,2,512]{2,1,0:T(2,128)S(1)} %get-tuple-element.45), channel_id=1, source_target_pairs={{8,0},{16,8},{24,16},{0,24},{9,1},{17,9},{25,17},{1,25},{10,2},{18... | collective-permute-start | bytes 24584 | tf_op jit(solution)/shard_map/ppermute | solution.py:20
  130.8 9.0 %collective-permute-start.30 = (f32[2,132,2]{2,1,0:T(8,128)S(1)}, f32[2,132,2]{2,1,0:T(8,128)S(1)}, u32[]{:S(2)}, u32[]{:S(2)}) collective-permute-start(f32[2,132,2]{2,1,0:T(8,128)S(1)} %get-tuple-element.12), channel_id=1, source_target_pairs={{0,1},{1,2},{2,3},{3,4},{4,5},{5,6},{6,7},{7,0},{8,9},{9,10},{10,1... | collective-permute-start | bytes 6344 | tf_op jit(solution)/shard_map/ppermute | solution.py:18
  131.0 10.2 %collective-permute-start.31 = (f32[2,132,2]{2,1,0:T(8,128)S(1)}, f32[2,132,2]{2,1,0:T(8,128)S(1)}, u32[]{:S(2)}, u32[]{:S(2)}) collective-permute-start(f32[2,132,2]{2,1,0:T(8,128)S(1)} %get-tuple-element.13), channel_id=1, source_target_pairs={{1,0},{2,1},{3,2},{4,3},{5,4},{6,5},{7,6},{0,7},{9,8},{10,9},{11,1... | collective-permute-start | bytes 6344 | tf_op jit(solution)/shard_map/ppermute | solution.py:20
